TPU v7x, 32 devices: a whole 2x2x4 slice. The times are simulated.
32 devices in a mesh: row: 8 (over z, y), col: 4 (over x, core).
Axes of the slice: x: 2, y: 2, z: 4, core: 2. Of those that a mesh axis runs over, the one named last changes fastest.
Arguments:
- front: bfloat16 [8192, 8192], P('row', 'col'), may hold values from -0.125 to 0.125
- tile_mask: int32 [32, 32], P('row', 'col'), may hold values 0 or 1
- probes: bfloat16 [8192, 256], P(('col', 'row')), may hold values from -6 to 6
- coupling: float32 [8192, 256], P(('row', 'col')), may hold values from -0.375 to 0.375
Outputs:
- leaf_basis: float32 [8192, 256], P(('row', 'col'))
- upper_transfer: float32 [4, 8192, 256], P(None, ('row', 'col'))
Inputs may be any that keep to these rules, and one draw needn't show every extreme that they name: `tile_mask`: 1 where a tile of the front is present, 0 where it is absent.
All inputs are finite; a program needn't handle non-finite values. No bound on the sum of `tile_mask` on one device may be relied on, other than what follows from the above.
Results may differ from a plain program's by a relative error of at most 0.0003.
Values may be sent and summed in bfloat16 or wider, within the bound.
No kernel may reach another device: no remote copies, remote signals or barrier semaphores. Data moves between devices by JAX's collectives and lax.ppermute only.
A program may use at most 128 MiB of HBM per device.

v0:
```python
import jax
import jax.numpy as jnp
from jax import lax
from jax.sharding import PartitionSpec as P


def from_root(x, axis, root):
    mine = lax.axis_index(axis) == root
    return lax.psum(jnp.where(mine, x, jnp.zeros_like(x)), axis)


def from_partner(value, axis, distance):
    mask = 2**distance
    pairs = [(source, source ^ mask) for source in range(lax.axis_size(axis))]
    return lax.ppermute(value, axis, pairs)


def matmul_high(left, right):
    return jnp.matmul(left, right, precision=lax.Precision.HIGHEST)


def transpose_last(array):
    return jnp.swapaxes(array, -1, -2)


def merge_pair(top_node, bottom_node, level_index):
    top_s, top_w, top_p = top_node
    bottom_s, bottom_w, bottom_p = bottom_node
    if level_index > 1:
        factor = 2.0 ** (-(level_index - 1) / 2.0)
        top_s = top_s - factor * matmul_high(top_p, bottom_w)
        bottom_s = bottom_s - factor * matmul_high(bottom_p, top_w)
    stacked = jnp.concatenate([top_s, bottom_s], axis=-2)
    gram_matrix = matmul_high(transpose_last(stacked), stacked)
    probe_count = gram_matrix.shape[-1]
    shift_value = 0.001 * (jnp.trace(gram_matrix, axis1=-2, axis2=-1) / probe_count + 1e-06)
    gram_matrix = gram_matrix + shift_value[..., None, None] * jnp.eye(
        probe_count, dtype=jnp.float32
    )
    lower_factor = jnp.linalg.cholesky(gram_matrix)
    basis_rows = jax.scipy.linalg.solve_triangular(
        lower_factor, transpose_last(stacked), lower=True
    )
    new_w = matmul_high(basis_rows, jnp.concatenate([top_w, bottom_w], axis=-2))
    row_total = top_s.shape[-2]
    top_half = transpose_last(basis_rows[..., :row_total])
    bottom_half = transpose_last(basis_rows[..., row_total:])
    return ((transpose_last(lower_factor), new_w, top_p + bottom_p), top_half, bottom_half)


def pair_step(node_state, partner, side_bit, level_index):
    is_top = side_bit == 0
    top_node = tuple((jnp.where(is_top, mine, other) for mine, other in zip(node_state, partner)))
    bottom_node = tuple(
        (jnp.where(is_top, other, mine) for mine, other in zip(node_state, partner))
    )
    parent, top_half, bottom_half = merge_pair(top_node, bottom_node, level_index)
    return (parent, jnp.where(is_top, top_half, bottom_half))


def pack_state(node_state):
    return jnp.concatenate(node_state, axis=0)


def unpack_state(packed, sample_rows, probe_rows):
    return (
        packed[:sample_rows],
        packed[sample_rows : sample_rows + probe_rows],
        packed[sample_rows + probe_rows :],
    )


def shards(front, tile_mask, probes, coupling):
    col_count = lax.axis_size("col")
    row_count = lax.axis_size("row")
    row_index = lax.axis_index("row")
    col_index = lax.axis_index("col")
    leaf_rows = front.shape[0] // col_count
    probe_count = probes.shape[1]
    col_levels = col_count.bit_length() - 1
    row_levels = row_count.bit_length() - 1
    probe_block = lax.all_gather(probes, "row", axis=0, tiled=True)
    tile_above = row_index * col_count + jnp.arange(col_count, dtype=jnp.int32)
    tile_across = col_index * row_count + jnp.arange(row_count, dtype=jnp.int32)
    keep_tiles = tile_mask * (tile_above[:, None] // 2 != tile_across[None, :] // 2).astype(
        jnp.int32
    )
    masked = (
        front.reshape(col_count, leaf_rows, row_count, leaf_rows)
        * keep_tiles.astype(jnp.bfloat16)[:, None, :, None]
    )
    partial_value = jnp.dot(
        masked.reshape(front.shape), probe_block, preferred_element_type=jnp.float32
    )
    sample = lax.psum_scatter(partial_value, "col", scatter_dimension=0, tiled=True)
    offset = row_index * col_count % row_count * leaf_rows
    root_col = row_index * col_count // row_count
    offered = lax.dynamic_slice_in_dim(probe_block, offset, col_count * leaf_rows, 0)
    group_probes = from_root(offered, "col", root_col)
    own_probe = lax.dynamic_slice_in_dim(group_probes, col_index * leaf_rows, leaf_rows, 0).astype(
        jnp.float32
    )
    halves = []
    node_state = (sample, own_probe, coupling)
    for bit_index in range(col_levels):
        sample_rows = node_state[0].shape[0]
        probe_rows = node_state[1].shape[0]
        packed = from_partner(pack_state(node_state), "col", bit_index)
        partner = unpack_state(packed, sample_rows, probe_rows)
        node_state, own_half = pair_step(
            node_state, partner, col_index >> bit_index & 1, bit_index + 1
        )
        halves.append(own_half)
    for bit_index in range(row_levels):
        packed = from_partner(pack_state(node_state), "row", bit_index)
        partner = unpack_state(packed, probe_count, probe_count)
        node_state, own_half = pair_step(
            node_state, partner, row_index >> bit_index & 1, col_levels + bit_index + 1
        )
        halves.append(own_half)
    return (halves[0], jnp.stack(halves[1:], axis=0))


def solution(mesh):
    in_specs = (P("row", "col"), P("row", "col"), P(("col", "row"), None), P(("row", "col"), None))
    out_specs = (P(("row", "col"), None), P(None, ("row", "col"), None))
    return jax.shard_map(shards, mesh=mesh, in_specs=in_specs, out_specs=out_specs, check_vma=False)
```

profile of v0, /device:TPU:0, one launch (start us, length us, event | category | flops | bytes accessed | tf_op | source)
XLA Modules:
  0.0 565.7 jit_solution(5704452580519430025)
XLA Ops:
  13.5 39.2 %all-gather.2.cloned.1.call-done = bf16[2048,256]{0,1:T(8,128)(2,1)} async-done(((bf16[256,256]{0,1:T(8,128)(2,1)}), bf16[2048,256]{0,1:T(8,128)(2,1)}) %all-gather.2.cloned.1.call-update) | async-done | bytes 1048592 | tf_op jit(solution)/shard_map/all_gather | solution.py:82
  61.1 26.4 %all-reduce.3.cloned.1.call-done = bf16[1024,256]{0,1:T(8,128)(2,1)} async-done(((bf16[1024,256]{0,1:T(8,128)(2,1)}), bf16[1024,256]{0,1:T(8,128)(2,1)}) %all-reduce.3.cloned.1.call-update) | async-done | bytes 524304 | tf_op jit(solution)/shard_map/psum | solution.py:9
  88.4 27.1 %reduce-scatter.2.cloned.1.call-done = f32[256,256]{0,1:T(8,128)} async-done(((f32[1024,256]{0,1:T(8,128)}), f32[256,256]{0,1:T(8,128)}) %reduce-scatter.2.cloned.1.call-update) | async-done | bytes 262160 | tf_op jit(solution)/shard_map/reduce_scatter | solution.py:95
  122.1 11.7 %cholesky.256 = f32[128,128]{1,0:T(8,128)S(1)} custom-call(f32[128,128]{1,0:T(8,128)S(1)} %cholesky.422), custom_call_target="Cholesky" | custom-call | tf_op jit(solution)/shard_map/jit(cholesky)/cholesky | solution.py:40
  144.5 12.1 %cholesky.273 = f32[128,128]{1,0:T(8,128)S(1)} custom-call(f32[128,128]{1,0:T(8,128)S(1)} %convolution_subtract_fusion.9), custom_call_target="Cholesky" | custom-call | tf_op jit(solution)/shard_map/jit(cholesky)/cholesky | solution.py:40
  162.9 19.7 %custom-call.20 = f32[2,128,128]{1,2,0:T(8,128)S(1)} custom-call(f32[2,128,128]{2,1,0:T(8,128)S(1)} %get-tuple-element.36), custom_call_target="InvertDiagBlocksLowerTriangular" | custom-call | tf_op jit(solution)/shard_map/jit(_solve_triangular)/triangular_solve | solution.py:41
  185.3 19.2 %collective-permute-done.1 = f32[768,256]{0,1:T(8,128)S(1)} collective-permute-done((f32[768,256]{0,1:T(8,128)S(1)}, f32[768,256]{0,1:T(8,128)S(1)}, u32[]{:S(2)}, u32[]{:S(2)}) %collective-permute-start.1) | collective-permute-done | bytes 786464 | tf_op jit(solution)/shard_map/ppermute | solution.py:15
  207.6 11.7 %cholesky.290 = f32[128,128]{1,0:T(8,128)S(1)} custom-call(f32[128,128]{1,0:T(8,128)S(1)} %cholesky.425), custom_call_target="Cholesky" | custom-call | tf_op jit(solution)/shard_map/jit(cholesky)/cholesky | solution.py:40
  219.4 9.8 %custom-call.21 = f32[1,128,128]{1,2,0:T(8,128)S(1)} custom-call(f32[1,128,128]{2,1,0:T(8,128)S(1)} %get-tuple-element.130), custom_call_target="InvertDiagBlocksLowerTriangular" | custom-call | tf_op jit(solution)/shard_map/jit(cholesky)/cholesky | solution.py:40
  229.9 11.9 %cholesky.307 = f32[128,128]{1,0:T(8,128)S(1)} custom-call(f32[128,128]{1,0:T(8,128)S(1)} %convolution_subtract_fusion.8), custom_call_target="Cholesky" | custom-call | tf_op jit(solution)/shard_map/jit(cholesky)/cholesky | solution.py:40
  248.5 19.7 %custom-call.22 = f32[2,128,128]{1,2,0:T(8,128)S(1)} custom-call(f32[2,128,128]{2,1,0:T(8,128)S(1)} %get-tuple-element.37), custom_call_target="InvertDiagBlocksLowerTriangular" | custom-call | tf_op jit(solution)/shard_map/jit(_solve_triangular)/triangular_solve | solution.py:41
  271.9 17.4 %collective-permute-done.2 = f32[768,256]{0,1:T(8,128)} collective-permute-done((f32[768,256]{0,1:T(8,128)S(1)}, f32[768,256]{0,1:T(8,128)}, u32[]{:S(2)}, u32[]{:S(2)}) %collective-permute-start.2) | collective-permute-done | bytes 786464 | tf_op jit(solution)/shard_map/ppermute | solution.py:15
  295.5 11.7 %cholesky.324 = f32[128,128]{1,0:T(8,128)S(1)} custom-call(f32[128,128]{1,0:T(8,128)S(1)} %cholesky.428), custom_call_target="Cholesky" | custom-call | tf_op jit(solution)/shard_map/jit(cholesky)/cholesky | solution.py:40
  307.2 9.8 %custom-call.23 = f32[1,128,128]{1,2,0:T(8,128)S(1)} custom-call(f32[1,128,128]{2,1,0:T(8,128)S(1)} %get-tuple-element.126), custom_call_target="InvertDiagBlocksLowerTriangular" | custom-call | tf_op jit(solution)/shard_map/jit(cholesky)/cholesky | solution.py:40
  317.7 12.1 %cholesky.341 = f32[128,128]{1,0:T(8,128)S(1)} custom-call(f32[128,128]{1,0:T(8,128)S(1)} %convolution_subtract_fusion.7), custom_call_target="Cholesky" | custom-call | tf_op jit(solution)/shard_map/jit(cholesky)/cholesky | solution.py:40
  336.5 19.7 %custom-call.24 = f32[2,128,128]{1,2,0:T(8,128)S(1)} custom-call(f32[2,128,128]{2,1,0:T(8,128)S(1)} %get-tuple-element.38), custom_call_target="InvertDiagBlocksLowerTriangular" | custom-call | tf_op jit(solution)/shard_map/jit(_solve_triangular)/triangular_solve | solution.py:41
  360.0 16.5 %collective-permute-done.3 = f32[768,256]{0,1:T(8,128)} collective-permute-done((f32[768,256]{0,1:T(8,128)S(1)}, f32[768,256]{0,1:T(8,128)}, u32[]{:S(2)}, u32[]{:S(2)}) %collective-permute-start.3) | collective-permute-done | bytes 786464 | tf_op jit(solution)/shard_map/ppermute | solution.py:15
  384.3 11.7 %cholesky.358 = f32[128,128]{1,0:T(8,128)S(1)} custom-call(f32[128,128]{1,0:T(8,128)S(1)} %cholesky.431), custom_call_target="Cholesky" | custom-call | tf_op jit(solution)/shard_map/jit(cholesky)/cholesky | solution.py:40
  408.3 11.9 %cholesky.375 = f32[128,128]{1,0:T(8,128)S(1)} custom-call(f32[128,128]{1,0:T(8,128)S(1)} %convolution_subtract_fusion.6), custom_call_target="Cholesky" | custom-call | tf_op jit(solution)/shard_map/jit(cholesky)/cholesky | solution.py:40
  429.3 20.5 %custom-call.26 = f32[2,128,128]{1,2,0:T(8,128)S(1)} custom-call(f32[2,128,128]{2,1,0:T(8,128)} %copy-done.7), custom_call_target="InvertDiagBlocksLowerTriangular" | custom-call | tf_op jit(solution)/shard_map/jit(_solve_triangular)/triangular_solve | solution.py:41
  460.7 29.8 %collective-permute-done.4 = f32[768,256]{0,1:T(8,128)} collective-permute-done((f32[768,256]{0,1:T(8,128)}, f32[768,256]{0,1:T(8,128)}, u32[]{:S(2)}, u32[]{:S(2)}) %collective-permute-start.4) | collective-permute-done | bytes 786464 | tf_op jit(solution)/shard_map/ppermute | solution.py:15
  495.8 11.7 %cholesky.392 = f32[128,128]{1,0:T(8,128)S(1)} custom-call(f32[128,128]{1,0:T(8,128)S(1)} %cholesky.434), custom_call_target="Cholesky" | custom-call | tf_op jit(solution)/shard_map/jit(cholesky)/cholesky | solution.py:40
  517.9 11.9 %cholesky.409 = f32[128,128]{1,0:T(8,128)S(1)} custom-call(f32[128,128]{1,0:T(8,128)S(1)} %convolution_subtract_fusion.5), custom_call_target="Cholesky" | custom-call | tf_op jit(solution)/shard_map/jit(cholesky)/cholesky | solution.py:40
  536.7 19.7 %custom-call.28 = f32[2,128,128]{1,2,0:T(8,128)S(1)} custom-call(f32[2,128,128]{2,1,0:T(8,128)S(1)} %get-tuple-element.40), custom_call_target="InvertDiagBlocksLowerTriangular" | custom-call | tf_op jit(solution)/shard_map/jit(_solve_triangular)/triangular_solve | solution.py:41
  (207 shorter events, 148.0 us)
Async XLA Ops:
  7.2 45.6 %all-gather.2.cloned.1.call-start = ((), (), s32[]{:S(2)}) async-start(), calls=%async_computation.1 | async-start | bytes 1179648 | tf_op jit(solution)/shard_map/all_gather | solution.py:82
  8.9 78.6 %all-reduce.3.cloned.1.call-start = ((), (), s32[]{:S(2)}) async-start(), calls=%async_computation.3 | async-start | bytes 1048576 | tf_op jit(solution)/shard_map/psum | solution.py:9
  54.7 60.8 %reduce-scatter.2.cloned.1.call-start = ((), (), s32[]{:S(2)}) async-start(), calls=%async_computation.2 | async-start | bytes 1310720 | tf_op jit(solution)/shard_map/reduce_scatter | solution.py:95
  55.0 6.0 %copy-start.6 = (f32[256,256]{1,0:T(8,128)S(1)}, f32[256,256]{1,0:T(8,128)}, u32[]{:S(2)}) copy-start(f32[256,256]{1,0:T(8,128)} %param.10) | copy-start | bytes 786436
  116.5 2.4 collective-permute-start
  184.8 19.7 %collective-permute-start.1 = (f32[768,256]{0,1:T(8,128)S(1)}, f32[768,256]{0,1:T(8,128)S(1)}, u32[]{:S(2)}, u32[]{:S(2)}) collective-permute-start(f32[768,256]{0,1:T(8,128)S(1)} %pad_maximum_fusion.2), channel_id=1, source_target_pairs={{0,2},{1,3},{2,0},{3,1},{4,6},{5,7},{6,4},{7,5},{8,10},{9,11},{10,... | collective-permute-start | bytes 2359304 | tf_op jit(solution)/shard_map/ppermute | solution.py:15
  270.4 18.9 %collective-permute-start.2 = (f32[768,256]{0,1:T(8,128)S(1)}, f32[768,256]{0,1:T(8,128)}, u32[]{:S(2)}, u32[]{:S(2)}) collective-permute-start(f32[768,256]{0,1:T(8,128)S(1)} %pad_maximum_fusion.3), channel_id=1, source_target_pairs={{0,4},{4,0},{8,12},{12,8},{16,20},{20,16},{24,28},{28,24},{1,5},{5... | collective-permute-start | bytes 2359304 | tf_op jit(solution)/shard_map/ppermute | solution.py:15
  358.5 18.0 %collective-permute-start.3 = (f32[768,256]{0,1:T(8,128)S(1)}, f32[768,256]{0,1:T(8,128)}, u32[]{:S(2)}, u32[]{:S(2)}) collective-permute-start(f32[768,256]{0,1:T(8,128)S(1)} %pad_maximum_fusion.4), channel_id=1, source_target_pairs={{0,8},{4,12},{8,0},{12,4},{16,24},{20,28},{24,16},{28,20},{1,9},{5... | collective-permute-start | bytes 2359304 | tf_op jit(solution)/shard_map/ppermute | solution.py:15
  384.3 11.8 %copy-start.5 = (f32[256,256]{1,0:T(8,128)}, f32[256,256]{1,0:T(8,128)S(1)}, u32[]{:S(2)}) copy-start(f32[256,256]{1,0:T(8,128)S(1)} %fusion.58) | copy-start | bytes 786436
  420.2 2.7 copy-start.1
  427.9 0.7 copy-start.7
  428.6 0.7 copy-start
  455.4 35.1 %collective-permute-start.4 = (f32[768,256]{0,1:T(8,128)}, f32[768,256]{0,1:T(8,128)}, u32[]{:S(2)}, u32[]{:S(2)}) collective-permute-start(f32[768,256]{0,1:T(8,128)} %pad_maximum_fusion.5), channel_id=1, source_target_pairs={{0,16},{4,20},{8,24},{12,28},{16,0},{20,4},{24,8},{28,12},{1,17},{... | collective-permute-start | bytes 2359304 | tf_op jit(solution)/shard_map/ppermute | solution.py:15
  494.8 63.1 %copy-start.2 = (f32[1,256,256]{2,1,0:T(8,128)S(1)}, f32[1,256,256]{2,1,0:T(8,128)}, u32[]{:S(2)}) copy-start(f32[1,256,256]{2,1,0:T(8,128)} %fusion.41) | copy-start | bytes 786436
  494.8 63.1 %copy-start.3 = (f32[1,256,256]{2,1,0:T(8,128)S(1)}, f32[1,256,256]{2,1,0:T(8,128)}, u32[]{:S(2)}) copy-start(f32[1,256,256]{2,1,0:T(8,128)} %fusion.37) | copy-start | bytes 786436
  494.8 63.1 %copy-start.4 = (f32[1,256,256]{2,1,0:T(8,128)S(1)}, f32[1,256,256]{2,1,0:T(8,128)}, u32[]{:S(2)}) copy-start(f32[1,256,256]{2,1,0:T(8,128)} %fusion.33) | copy-start | bytes 786436
Sparse Core Ops, SparseCore 0:
  10.6 42.1 all-gather.1
  55.1 32.3 all-reduce.2
  90.6 24.8 reduce-scatter.1
where the time goes:
time: 569 us; the launch traced here: 566 us
  other arithmetic  289 us (51%)
  waiting for transfers between devices  178 us (31%)
  matrix products  38.1 us (7%)
  local copies, waits for them, and re-layouts  29.5 us (5%)
  between operations  25 us (4%)
  starting transfers between devices  6.23 us (1%)
    another operation x34, other arithmetic, merge_pair(): lower_factor = jnp.linalg.cholesky(gram_matrix)  174 us
    another operation x10, other arithmetic, merge_pair(): jax.scipy.linalg.solve_triangular(lower_factor, transpose_last(stacked),...  100 us
    ppermute x5, waiting for transfers between devices, from_partner(): return lax.ppermute(value, axis, pairs)  85.1 us
    all_gather x1, waiting for transfers between devices, shards(): probe_block = lax.all_gather(probes, 'row', axis=0, tiled=True)  39.2 us
    reduce_scatter x1, waiting for transfers between devices, shards(): lax.psum_scatter(partial_value, 'col', scatter_dimension=0, tiled=True)  27.1 us
    psum x1, waiting for transfers between devices, from_root(): return lax.psum(jnp.where(mine, x, jnp.zeros_like(x)), axis)  26.4 us
    another operation x41, local copies, waits for them, and re-layouts, merge_pair(): jax.scipy.linalg.solve_triangular(lower_factor, transpose_last(stacked),...  20.7 us
    dot_general x17, matrix products, matmul_high(): return jnp.matmul(left, right, precision=lax.Precision.HIGHEST)  18.2 us
  transfers between devices with their start and end apart: 8, of which 8 were waited for; matrix products, arithmetic and copies ran while one was open for 3% of the time, Pallas kernels for 0%

commit v1 on v0

--- a/solution.py
+++ b/solution.py
@@ -79,7 +79,15 @@
     probe_count = probes.shape[1]
     col_levels = col_count.bit_length() - 1
     row_levels = row_count.bit_length() - 1
-    probe_block = lax.all_gather(probes, "row", axis=0, tiled=True)
+    probe_block = jnp.concatenate(
+        lax.all_to_all(
+            jnp.stack([probes] * lax.axis_size("row"), 0),
+            axis_name="row",
+            split_axis=0,
+            concat_axis=0,
+        ),
+        axis=0,
+    )
     tile_above = row_index * col_count + jnp.arange(col_count, dtype=jnp.int32)
     tile_across = col_index * row_count + jnp.arange(row_count, dtype=jnp.int32)
     keep_tiles = tile_mask * (tile_above[:, None] // 2 != tile_across[None, :] // 2).astype(

time: 569 us -> 558 us (0.981)
  waiting for transfers between devices: 178 us -> 160 us
  starting transfers between devices: 6.23 us -> 13.5 us
    all_gather x1 -> x0, waiting for transfers between devices: 39.2 us -> none  [shards(): probe_block = lax.all_gather(probes, 'row', axis=0, tiled=True)]
    all_to_all x0 -> x1, waiting for transfers between devices: none -> 21.2 us  [shards(): lax.all_to_all(jnp.stack([probes] * lax.axis_size('row'), 0), axis_name='...]
    all_to_all x0 -> x1, starting transfers between devices: none -> 7.31 us  [shards(): lax.all_to_all(jnp.stack([probes] * lax.axis_size('row'), 0), axis_name='...]
where the time goes in v1:
time: 558 us; the launch traced here: 554 us
  other arithmetic  288 us (52%)
  waiting for transfers between devices  160 us (29%)
  matrix products  37.9 us (7%)
  local copies, waits for them, and re-layouts  30 us (5%)
  between operations  25.3 us (5%)
  starting transfers between devices  13.5 us (2%)
    another operation x34, other arithmetic, merge_pair(): lower_factor = jnp.linalg.cholesky(gram_matrix)  174 us
    another operation x10, other arithmetic, merge_pair(): jax.scipy.linalg.solve_triangular(lower_factor, transpose_last(stacked),...  100 us
    ppermute x5, waiting for transfers between devices, from_partner(): return lax.ppermute(value, axis, pairs)  85.1 us
    reduce_scatter x1, waiting for transfers between devices, shards(): lax.psum_scatter(partial_value, 'col', scatter_dimension=0, tiled=True)  27.1 us
    psum x1, waiting for transfers between devices, from_root(): return lax.psum(jnp.where(mine, x, jnp.zeros_like(x)), axis)  26.4 us
    all_to_all x1, waiting for transfers between devices, shards(): lax.all_to_all(jnp.stack([probes] * lax.axis_size('row'), 0), axis_name='...  21.2 us
    another operation x41, local copies, waits for them, and re-layouts, merge_pair(): jax.scipy.linalg.solve_triangular(lower_factor, transpose_last(stacked),...  20.7 us
    dot_general x17, matrix products, matmul_high(): return jnp.matmul(left, right, precision=lax.Precision.HIGHEST)  18.2 us
  transfers between devices with their start and end apart: 8, of which 8 were waited for; matrix products, arithmetic and copies ran while one was open for 3% of the time, Pallas kernels for 0%

profile of v1, /device:TPU:0, one launch (start us, length us, event | category | flops | bytes accessed | tf_op | source)
XLA Modules:
  0.0 554.5 jit_solution(3363246605068466303)
XLA Ops:
  21.1 21.2 %all-to-all-done = bf16[8,256,256]{1,2,0:T(8,128)(2,1)S(1)} async-done(((bf16[8,256,256]{1,2,0:T(8,128)(2,1)}), bf16[8,256,256]{1,2,0:T(8,128)(2,1)S(1)}, u32[]{:S(2)}, u32[]{:S(2)}) %all-to-all-start) | async-done | bytes 1048608 | tf_op jit(solution)/shard_map/all_to_all | solution.py:83
  49.6 26.4 %all-reduce.3.cloned.1.call-done = bf16[1024,256]{0,1:T(8,128)(2,1)} async-done(((bf16[1024,256]{0,1:T(8,128)(2,1)}), bf16[1024,256]{0,1:T(8,128)(2,1)}) %all-reduce.3.cloned.1.call-update) | async-done | bytes 524304 | tf_op jit(solution)/shard_map/psum | solution.py:9
  76.9 27.1 %reduce-scatter.2.cloned.1.call-done = f32[256,256]{0,1:T(8,128)} async-done(((f32[1024,256]{0,1:T(8,128)}), f32[256,256]{0,1:T(8,128)}) %reduce-scatter.2.cloned.1.call-update) | async-done | bytes 262160 | tf_op jit(solution)/shard_map/reduce_scatter | solution.py:103
  110.6 11.7 %cholesky.256 = f32[128,128]{1,0:T(8,128)S(1)} custom-call(f32[128,128]{1,0:T(8,128)S(1)} %cholesky.422), custom_call_target="Cholesky" | custom-call | tf_op jit(solution)/shard_map/jit(cholesky)/cholesky | solution.py:40
  122.3 9.8 %custom-call.19 = f32[1,128,128]{1,2,0:T(8,128)S(1)} custom-call(f32[1,128,128]{2,1,0:T(8,128)S(1)} %get-tuple-element.134), custom_call_target="InvertDiagBlocksLowerTriangular" | custom-call | tf_op jit(solution)/shard_map/jit(cholesky)/cholesky | solution.py:40
  132.9 12.1 %cholesky.273 = f32[128,128]{1,0:T(8,128)S(1)} custom-call(f32[128,128]{1,0:T(8,128)S(1)} %convolution_subtract_fusion.9), custom_call_target="Cholesky" | custom-call | tf_op jit(solution)/shard_map/jit(cholesky)/cholesky | solution.py:40
  151.4 19.7 %custom-call.20 = f32[2,128,128]{1,2,0:T(8,128)S(1)} custom-call(f32[2,128,128]{2,1,0:T(8,128)S(1)} %get-tuple-element.36), custom_call_target="InvertDiagBlocksLowerTriangular" | custom-call | tf_op jit(solution)/shard_map/jit(_solve_triangular)/triangular_solve | solution.py:41
  173.7 19.2 %collective-permute-done.1 = f32[768,256]{0,1:T(8,128)S(1)} collective-permute-done((f32[768,256]{0,1:T(8,128)S(1)}, f32[768,256]{0,1:T(8,128)S(1)}, u32[]{:S(2)}, u32[]{:S(2)}) %collective-permute-start.1) | collective-permute-done | bytes 786464 | tf_op jit(solution)/shard_map/ppermute | solution.py:15
  196.1 11.7 %cholesky.290 = f32[128,128]{1,0:T(8,128)S(1)} custom-call(f32[128,128]{1,0:T(8,128)S(1)} %cholesky.425), custom_call_target="Cholesky" | custom-call | tf_op jit(solution)/shard_map/jit(cholesky)/cholesky | solution.py:40
  207.8 9.8 %custom-call.21 = f32[1,128,128]{1,2,0:T(8,128)S(1)} custom-call(f32[1,128,128]{2,1,0:T(8,128)S(1)} %get-tuple-element.130), custom_call_target="InvertDiagBlocksLowerTriangular" | custom-call | tf_op jit(solution)/shard_map/jit(cholesky)/cholesky | solution.py:40
  218.3 11.9 %cholesky.307 = f32[128,128]{1,0:T(8,128)S(1)} custom-call(f32[128,128]{1,0:T(8,128)S(1)} %convolution_subtract_fusion.8), custom_call_target="Cholesky" | custom-call | tf_op jit(solution)/shard_map/jit(cholesky)/cholesky | solution.py:40
  236.9 19.7 %custom-call.22 = f32[2,128,128]{1,2,0:T(8,128)S(1)} custom-call(f32[2,128,128]{2,1,0:T(8,128)S(1)} %get-tuple-element.37), custom_call_target="InvertDiagBlocksLowerTriangular" | custom-call | tf_op jit(solution)/shard_map/jit(_solve_triangular)/triangular_solve | solution.py:41
  260.4 17.4 %collective-permute-done.2 = f32[768,256]{0,1:T(8,128)} collective-permute-done((f32[768,256]{0,1:T(8,128)S(1)}, f32[768,256]{0,1:T(8,128)}, u32[]{:S(2)}, u32[]{:S(2)}) %collective-permute-start.2) | collective-permute-done | bytes 786464 | tf_op jit(solution)/shard_map/ppermute | solution.py:15
  283.9 11.7 %cholesky.324 = f32[128,128]{1,0:T(8,128)S(1)} custom-call(f32[128,128]{1,0:T(8,128)S(1)} %cholesky.428), custom_call_target="Cholesky" | custom-call | tf_op jit(solution)/shard_map/jit(cholesky)/cholesky | solution.py:40
  306.2 12.1 %cholesky.341 = f32[128,128]{1,0:T(8,128)S(1)} custom-call(f32[128,128]{1,0:T(8,128)S(1)} %convolution_subtract_fusion.7), custom_call_target="Cholesky" | custom-call | tf_op jit(solution)/shard_map/jit(cholesky)/cholesky | solution.py:40
  325.0 19.7 %custom-call.24 = f32[2,128,128]{1,2,0:T(8,128)S(1)} custom-call(f32[2,128,128]{2,1,0:T(8,128)S(1)} %get-tuple-element.38), custom_call_target="InvertDiagBlocksLowerTriangular" | custom-call | tf_op jit(solution)/shard_map/jit(_solve_triangular)/triangular_solve | solution.py:41
  348.4 16.5 %collective-permute-done.3 = f32[768,256]{0,1:T(8,128)} collective-permute-done((f32[768,256]{0,1:T(8,128)S(1)}, f32[768,256]{0,1:T(8,128)}, u32[]{:S(2)}, u32[]{:S(2)}) %collective-permute-start.3) | collective-permute-done | bytes 786464 | tf_op jit(solution)/shard_map/ppermute | solution.py:15
  372.8 11.7 %cholesky.358 = f32[128,128]{1,0:T(8,128)S(1)} custom-call(f32[128,128]{1,0:T(8,128)S(1)} %cholesky.431), custom_call_target="Cholesky" | custom-call | tf_op jit(solution)/shard_map/jit(cholesky)/cholesky | solution.py:40
  396.7 11.9 %cholesky.375 = f32[128,128]{1,0:T(8,128)S(1)} custom-call(f32[128,128]{1,0:T(8,128)S(1)} %convolution_subtract_fusion.6), custom_call_target="Cholesky" | custom-call | tf_op jit(solution)/shard_map/jit(cholesky)/cholesky | solution.py:40
  417.7 20.5 %custom-call.26 = f32[2,128,128]{1,2,0:T(8,128)S(1)} custom-call(f32[2,128,128]{2,1,0:T(8,128)} %copy-done.7), custom_call_target="InvertDiagBlocksLowerTriangular" | custom-call | tf_op jit(solution)/shard_map/jit(_solve_triangular)/triangular_solve | solution.py:41
  449.2 29.7 %collective-permute-done.4 = f32[768,256]{0,1:T(8,128)} collective-permute-done((f32[768,256]{0,1:T(8,128)}, f32[768,256]{0,1:T(8,128)}, u32[]{:S(2)}, u32[]{:S(2)}) %collective-permute-start.4) | collective-permute-done | bytes 786464 | tf_op jit(solution)/shard_map/ppermute | solution.py:15
  484.2 11.7 %cholesky.392 = f32[128,128]{1,0:T(8,128)S(1)} custom-call(f32[128,128]{1,0:T(8,128)S(1)} %cholesky.434), custom_call_target="Cholesky" | custom-call | tf_op jit(solution)/shard_map/jit(cholesky)/cholesky | solution.py:40
  506.3 11.9 %cholesky.409 = f32[128,128]{1,0:T(8,128)S(1)} custom-call(f32[128,128]{1,0:T(8,128)S(1)} %convolution_subtract_fusion.5), custom_call_target="Cholesky" | custom-call | tf_op jit(solution)/shard_map/jit(cholesky)/cholesky | solution.py:40
  525.1 19.7 %custom-call.28 = f32[2,128,128]{1,2,0:T(8,128)S(1)} custom-call(f32[2,128,128]{2,1,0:T(8,128)S(1)} %get-tuple-element.40), custom_call_target="InvertDiagBlocksLowerTriangular" | custom-call | tf_op jit(solution)/shard_map/jit(_solve_triangular)/triangular_solve | solution.py:41
  (208 shorter events, 154.5 us)
Async XLA Ops:
  9.2 33.1 %all-to-all-start = ((bf16[8,256,256]{1,2,0:T(8,128)(2,1)}), bf16[8,256,256]{1,2,0:T(8,128)(2,1)S(1)}, u32[]{:S(2)}, u32[]{:S(2)}) async-start(bf16[8,256,256]{1,2,0:T(8,128)(2,1)} %stack.12), calls=%async_computation | async-start | bytes 2097152 | tf_op jit(solution)/shard_map/all_to_all | solution.py:83
  16.5 59.4 %all-reduce.3.cloned.1.call-start = ((), (), s32[]{:S(2)}) async-start(), calls=%async_computation.3 | async-start | bytes 1048576 | tf_op jit(solution)/shard_map/psum | solution.py:9
  43.4 60.6 %reduce-scatter.2.cloned.1.call-start = ((), (), s32[]{:S(2)}) async-start(), calls=%async_computation.2 | async-start | bytes 1310720 | tf_op jit(solution)/shard_map/reduce_scatter | solution.py:103
  43.6 5.8 %copy-start.6 = (f32[256,256]{1,0:T(8,128)S(1)}, f32[256,256]{1,0:T(8,128)}, u32[]{:S(2)}) copy-start(f32[256,256]{1,0:T(8,128)} %param.10) | copy-start | bytes 786436
  105.0 2.4 collective-permute-start
  173.3 19.7 %collective-permute-start.1 = (f32[768,256]{0,1:T(8,128)S(1)}, f32[768,256]{0,1:T(8,128)S(1)}, u32[]{:S(2)}, u32[]{:S(2)}) collective-permute-start(f32[768,256]{0,1:T(8,128)S(1)} %pad_maximum_fusion.2), channel_id=1, source_target_pairs={{0,2},{1,3},{2,0},{3,1},{4,6},{5,7},{6,4},{7,5},{8,10},{9,11},{10,... | collective-permute-start | bytes 2359304 | tf_op jit(solution)/shard_map/ppermute | solution.py:15
  258.8 18.9 %collective-permute-start.2 = (f32[768,256]{0,1:T(8,128)S(1)}, f32[768,256]{0,1:T(8,128)}, u32[]{:S(2)}, u32[]{:S(2)}) collective-permute-start(f32[768,256]{0,1:T(8,128)S(1)} %pad_maximum_fusion.3), channel_id=1, source_target_pairs={{0,4},{4,0},{8,12},{12,8},{16,20},{20,16},{24,28},{28,24},{1,5},{5... | collective-permute-start | bytes 2359304 | tf_op jit(solution)/shard_map/ppermute | solution.py:15
  346.9 18.0 %collective-permute-start.3 = (f32[768,256]{0,1:T(8,128)S(1)}, f32[768,256]{0,1:T(8,128)}, u32[]{:S(2)}, u32[]{:S(2)}) collective-permute-start(f32[768,256]{0,1:T(8,128)S(1)} %pad_maximum_fusion.4), channel_id=1, source_target_pairs={{0,8},{4,12},{8,0},{12,4},{16,24},{20,28},{24,16},{28,20},{1,9},{5... | collective-permute-start | bytes 2359304 | tf_op jit(solution)/shard_map/ppermute | solution.py:15
  372.7 11.8 %copy-start.5 = (f32[256,256]{1,0:T(8,128)}, f32[256,256]{1,0:T(8,128)S(1)}, u32[]{:S(2)}) copy-start(f32[256,256]{1,0:T(8,128)S(1)} %fusion.58) | copy-start | bytes 786436
  408.6 2.7 copy-start.1
  416.4 0.7 copy-start.7
  417.0 0.7 copy-start
  443.8 35.1 %collective-permute-start.4 = (f32[768,256]{0,1:T(8,128)}, f32[768,256]{0,1:T(8,128)}, u32[]{:S(2)}, u32[]{:S(2)}) collective-permute-start(f32[768,256]{0,1:T(8,128)} %pad_maximum_fusion.5), channel_id=1, source_target_pairs={{0,16},{4,20},{8,24},{12,28},{16,0},{20,4},{24,8},{28,12},{1,17},{... | collective-permute-start | bytes 2359304 | tf_op jit(solution)/shard_map/ppermute | solution.py:15
  483.2 63.1 %copy-start.2 = (f32[1,256,256]{2,1,0:T(8,128)S(1)}, f32[1,256,256]{2,1,0:T(8,128)}, u32[]{:S(2)}) copy-start(f32[1,256,256]{2,1,0:T(8,128)} %fusion.41) | copy-start | bytes 786436
  483.2 63.1 %copy-start.3 = (f32[1,256,256]{2,1,0:T(8,128)S(1)}, f32[1,256,256]{2,1,0:T(8,128)}, u32[]{:S(2)}) copy-start(f32[1,256,256]{2,1,0:T(8,128)} %fusion.37) | copy-start | bytes 786436
  483.2 63.1 %copy-start.4 = (f32[1,256,256]{2,1,0:T(8,128)S(1)}, f32[1,256,256]{2,1,0:T(8,128)}, u32[]{:S(2)}) copy-start(f32[1,256,256]{2,1,0:T(8,128)} %fusion.33) | copy-start | bytes 786436
Sparse Core Ops, SparseCore 0:
  43.5 32.4 all-reduce.2
  79.1 24.8 reduce-scatter.1
